TPU v7x, 512 devices: a whole 4x4x16 slice. The times are simulated.
512 devices in a mesh: wide: 64 (over y, z_lo, core), narrow: 8 (over x, z_hi).
Axes of the slice: x: 4, y: 4, z: 16 (z_hi: 2, z_lo: 8; z = z_hi * 8 + z_lo), core: 2. Of those that a mesh axis runs over, the one named last changes fastest.
Arguments:
- tensor: bfloat16 [16, 4096, 8192], P('narrow', 'wide'), may hold values from -16 to 16
- factor_a: bfloat16 [32, 4096], P(None, 'wide'), may hold values from -0.21875 to 0.21875
- factor_b: bfloat16 [32, 8192], P(None, 'wide'), may hold values from -0.15625 to 0.15625
- factor_c: bfloat16 [32, 16], P(None, 'narrow'), may hold values from -4 to 4
Outputs:
- step_a: float32 [32, 4096], P(None, 'wide')
- step_b: float32 [32, 8192], P(None, 'wide')
- step_c: float32 [32, 16], P(None, 'narrow')
All inputs are finite; a program needn't handle non-finite values.
Results may differ from a plain program's by a relative error of at most 0.0029.
Values may be sent and summed in bfloat16 or wider, within the bound.
No kernel may reach another device: no remote copies, remote signals or barrier semaphores. Data moves between devices by JAX's collectives and lax.ppermute only.
A program may use at most 64 MiB of HBM per device.

v0:
```python
import jax
import jax.numpy as jnp
from jax import lax
from jax.sharding import PartitionSpec as P

ITERS = 2
damping = 1.0
highest = lax.Precision.HIGHEST


def matmul(left, right):
    return jnp.dot(left, right, precision=highest)


def outer_rows(left, right):
    return lax.dot_general(left, right, (((1,), (1,)), ((), ())), precision=highest)


def combine_dot(wide_part, narrow_part):
    return lax.psum(wide_part, "wide") + lax.psum(narrow_part, "narrow")


def self_inner(triple):
    return combine_dot(
        jnp.sum(triple[0] * triple[0]) + jnp.sum(triple[1] * triple[1]),
        jnp.sum(triple[2] * triple[2]),
    )


def gram_product(factors, grams, directions):
    float_a, float_b, float_c = factors
    gram_a, gram_b, gram_c = grams
    dir_a, dir_b, dir_c = directions
    local_a = outer_rows(float_a, dir_a)
    local_b = outer_rows(float_b, dir_b)
    local_c = outer_rows(float_c, dir_c)
    cross_a, cross_b = lax.psum((local_a, local_b), "wide")
    cross_c = lax.psum(local_c, "narrow")
    hadamard_a = gram_b * gram_c
    hadamard_b = gram_a * gram_c
    hadamard_c = gram_a * gram_b
    mixed_a = cross_b * gram_c + gram_b * cross_c
    mixed_b = cross_a * gram_c + gram_a * cross_c
    mixed_c = cross_a * gram_b + gram_a * cross_b
    image_a = matmul(hadamard_a, dir_a) + matmul(mixed_a, float_a) + damping * dir_a
    image_b = matmul(hadamard_b, dir_b) + matmul(mixed_b, float_b) + damping * dir_b
    image_c = matmul(hadamard_c, dir_c) + matmul(mixed_c, float_c) + damping * dir_c
    curvature = combine_dot(
        jnp.sum(dir_a * image_a) + jnp.sum(dir_b * image_b), jnp.sum(dir_c * image_c)
    )
    return ((image_a, image_b, image_c), curvature)


def on_device(tensor, factor_a, factor_b, factor_c):
    k_local, i_local, j_whole = tensor.shape
    rank = factor_a.shape[0]
    j_local = factor_b.shape[1]
    flattened = tensor.reshape(k_local * i_local, j_whole)
    contracted = lax.dot_general(
        lax.all_gather(factor_b, "wide", axis=1, tiled=True),
        flattened,
        (((1,), (1,)), ((), ())),
        preferred_element_type=jnp.float32,
    ).reshape(rank, k_local, i_local)
    float_a = factor_a.astype(jnp.float32)
    float_b = factor_b.astype(jnp.float32)
    float_c = factor_c.astype(jnp.float32)
    part_a = jnp.einsum("rk,rki->ri", float_c, contracted, precision=highest)
    part_c = jnp.einsum("ri,rki->rk", float_a, contracted, precision=highest)
    own_gram_a = jnp.dot(factor_a, factor_a.T, preferred_element_type=jnp.float32)
    own_gram_b = jnp.dot(factor_b, factor_b.T, preferred_element_type=jnp.float32)
    own_gram_c = jnp.dot(factor_c, factor_c.T, preferred_element_type=jnp.float32)
    mttkrp_a, gram_c = lax.psum((part_a, own_gram_c), "narrow")
    mttkrp_c, gram_a, gram_b = lax.psum((part_c, own_gram_a, own_gram_b), "wide")
    khatri = (
        (float_c[:, :, None] * float_a[:, None, :])
        .reshape(rank, k_local * i_local)
        .astype(jnp.bfloat16)
    )
    partial_b = jnp.dot(khatri, flattened, preferred_element_type=jnp.float32)
    total_b = lax.psum(partial_b, ("wide", "narrow"))
    mttkrp_b = lax.dynamic_slice_in_dim(total_b, lax.axis_index("wide") * j_local, j_local, 1)
    grad_a = matmul(gram_b * gram_c, float_a) - mttkrp_a
    grad_b = matmul(gram_a * gram_c, float_b) - mttkrp_b
    grad_c = matmul(gram_a * gram_b, float_c) - mttkrp_c
    factors = (float_a, float_b, float_c)
    grams = (gram_a, gram_b, gram_c)
    resid = (-grad_a, -grad_b, -grad_c)
    direction = resid
    steps = (jnp.zeros_like(grad_a), jnp.zeros_like(grad_b), jnp.zeros_like(grad_c))
    norm_now = self_inner(resid)
    for iteration in range(ITERS):
        image, curvature = gram_product(factors, grams, direction)
        step_size = norm_now / curvature
        steps = tuple((old + step_size * move for old, move in zip(steps, direction)))
        if iteration + 1 < ITERS:
            resid = tuple((old - step_size * move for old, move in zip(resid, image)))
            norm_next = self_inner(resid)
            momentum = norm_next / norm_now
            direction = tuple((now + momentum * old for now, old in zip(resid, direction)))
            norm_now = norm_next
    return (steps[0], steps[1], steps[2])


def solution(mesh):
    placed = (P("narrow", "wide", None), P(None, "wide"), P(None, "wide"), P(None, "narrow"))
    return jax.shard_map(
        on_device,
        mesh=mesh,
        in_specs=placed,
        out_specs=(P(None, "wide"), P(None, "wide"), P(None, "narrow")),
        check_vma=False,
    )
```

profile of v0, /device:TPU:1, one launch (start us, length us, event | category | flops | bytes accessed | tf_op | source)
XLA Modules:
  0.0 2312.1 jit_solution(18251631645562315056)
XLA Ops:
  7.2 0.8 convert_element_type.12
  8.1 0.7 convert_element_type.11
  8.8 1.6 convolution_bitcast_fusion
  10.6 129.4 %all_gather.3 = bf16[32,8192]{1,0:T(8,128)(2,1)S(1)} all-gather(bf16[32,128]{1,0:T(8,128)(2,1)S(1)} %copy-done.1), channel_id=1, replica_groups=mesh['wide'=64,'narrow'=8] {'wide'}, dimensions={1}, use_global_device_ids=true | all-gather | bytes 532480 | tf_op jit(solution)/shard_map/all_gather | solution.py:60
  140.3 1.1 fusion.12
  141.4 0.3 fusion.16
  141.7 0.2 fusion.14
  141.9 66.7 %all-reduce.6 = (f32[32,32]{1,0:T(8,128)S(1)}, f32[32,64]{1,0:T(8,128)S(1)}) all-reduce(f32[32,32]{1,0:T(8,128)S(1)} %fusion.51, f32[32,64]{1,0:T(8,128)S(1)} %bitcast.63), channel_id=1, replica_groups=mesh['wide'=64,'narrow'=8] {'narrow'}, use_global_device_ids=true, to_apply=%region_1.0 | all-reduce | flops 3072 | bytes 24576 | tf_op jit(solution)/shard_map/psum | solution.py:73
  208.7 415.4 %all-reduce.3 = (f32[32,32]{1,0:T(8,128)S(1)}, f32[32,32]{1,0:T(8,128)S(1)}) all-reduce(f32[32,32]{1,0:T(8,128)S(1)} %fusion.50, f32[32,32]{1,0:T(8,128)S(1)} %fusion.52), channel_id=1, replica_groups=mesh['wide'=64,'narrow'=8] {'wide'}, use_global_device_ids=true, to_apply=%region_0.0 | all-reduce | flops 2048 | bytes 16384 | tf_op jit(solution)/shard_map/psum | solution.py:74
  624.6 0.8 convolution_subtract_fusion
  625.7 418.8 %all-reduce.2 = (f32[32,2]{0,1:T(2,128)S(1)}, f32[32,32]{1,0:T(8,128)S(1)}, f32[32,32]{1,0:T(8,128)S(1)}) all-reduce(f32[32,2]{0,1:T(2,128)S(1)} %bitcast.64, f32[32,32]{1,0:T(8,128)S(1)} %convolution_bitcast_fusion.6, f32[32,32]{1,0:T(8,128)S(1)} %convolution_bitcast_fusion.4), channel_id=1, replica_groups=mesh['wide'=64,'narrow'=8] {'wide'}, use_global_device_ids=true, to_apply=%region_8.0 | all-reduce | flops 2112 | bytes 16896 | tf_op jit(solution)/shard_map/psum | solution.py:74
  1044.6 0.2 convolution_bitcast_fusion.5
  1045.0 0.8 multiply_reduce_fusion.7
  1045.7 60.0 %all-reduce.5 = (f32[32,32]{1,0:T(8,128)S(1)}, f32[]{:T(128)}, f32[]{:T(128)}) all-reduce(f32[32,32]{1,0:T(8,128)S(1)} %convolution_bitcast_fusion.5, f32[]{:T(128)} %get-tuple-element.8, f32[]{:T(128)} %get-tuple-element.7), channel_id=1, replica_groups=mesh['wide'=64,'narrow'=8] {'narrow'}, use_global_device_ids=true, to_apply=%region_12.0 | all-reduce | flops 1026 | bytes 8208 | tf_op jit(solution)/shard_map/psum | solution.py:38
  1105.8 0.8 multiply_reduce_fusion.3
  1106.6 0.8 multiply_reduce_fusion.2
  1109.9 228.5 %all-reduce.1 = (f32[]{:T(128)}, f32[]{:T(128)}) all-reduce(f32[]{:T(128)S(6)} %add.140, f32[]{:T(128)S(6)} %add.148), channel_id=1, replica_groups=mesh['wide'=64,'narrow'=8] {'wide'}, use_global_device_ids=true, to_apply=%region_7.0 | all-reduce | flops 2 | bytes 16 | tf_op jit(solution)/shard_map/psum | solution.py:20
  1341.1 0.6 multiply_reduce_fusion.1
  1341.7 0.6 multiply_reduce_fusion
  1343.6 0.6 multiply_reduce_fusion.6
  1344.2 210.8 %psum.153 = f32[]{:T(128)} all-reduce(f32[]{:T(128)S(6)} %add.153), channel_id=1, replica_groups=mesh['wide'=64,'narrow'=8] {'wide'}, use_global_device_ids=true, to_apply=%region_21.0 | all-reduce | flops 1 | bytes 8 | tf_op jit(solution)/shard_map/psum | solution.py:20
  1555.0 38.4 %psum.154 = f32[]{:T(128)} all-reduce(f32[]{:T(128)} %multiply_reduce_fusion.6), channel_id=1, replica_groups=mesh['wide'=64,'narrow'=8] {'narrow'}, use_global_device_ids=true, to_apply=%region_23.0 | all-reduce | flops 1 | bytes 8 | tf_op jit(solution)/shard_map/psum | solution.py:20
  1595.4 0.2 convolution_bitcast_fusion.2
  1595.6 412.3 %all-reduce = (f32[32,32]{1,0:T(8,128)S(1)}, f32[32,32]{1,0:T(8,128)S(1)}) all-reduce(f32[32,32]{1,0:T(8,128)S(1)} %convolution_bitcast_fusion.3, f32[32,32]{1,0:T(8,128)S(1)} %convolution_bitcast_fusion.1), channel_id=1, replica_groups=mesh['wide'=64,'narrow'=8] {'wide'}, use_global_device_ids=true, to_apply=%region_24.0 | all-reduce | flops 2048 | bytes 16384 | tf_op jit(solution)/shard_map/psum | solution.py:37
  2008.0 0.8 fusion.11
  2008.8 62.2 %all-reduce.4 = (f32[32,32]{1,0:T(8,128)S(1)}, f32[]{:T(128)}) all-reduce(f32[32,32]{1,0:T(8,128)S(1)} %convolution_bitcast_fusion.2, f32[]{:T(128)} %fusion.11), channel_id=1, replica_groups=mesh['wide'=64,'narrow'=8] {'narrow'}, use_global_device_ids=true, to_apply=%region_25.0 | all-reduce | flops 1025 | bytes 8200 | tf_op jit(solution)/shard_map/psum | solution.py:38
  2071.0 0.7 fusion.9
  2071.7 0.7 fusion.10
  2073.7 228.4 %psum.158 = f32[]{:T(128)} all-reduce(f32[]{:T(128)S(6)} %add.164), channel_id=1, replica_groups=mesh['wide'=64,'narrow'=8] {'wide'}, use_global_device_ids=true, to_apply=%region_29.0 | all-reduce | flops 1 | bytes 8 | tf_op jit(solution)/shard_map/psum | solution.py:20
  2303.5 0.6 multiply_add_fusion.1
  2304.1 0.6 multiply_add_fusion
  2304.7 0.6 multiply_add_fusion.4
  (32 shorter events, 2.4 us)
Async XLA Ops:
  7.2 1.6 copy-start
  7.2 617.4 %all-reduce.9.cloned.1.call-start = ((), (), s32[]{:S(2)}) async-start(), calls=%async_computation | async-start | bytes 2097152 | tf_op jit(solution)/shard_map/psum | solution.py:81
  8.8 1.6 copy-start.3
  8.8 1.8 copy-start.1
  8.8 131.3 %copy-start.2 = (bf16[32,64]{1,0:T(8,128)(2,1)S(1)}, bf16[32,64]{1,0:T(8,128)(2,1)}, u32[]{:S(2)}) copy-start(bf16[32,64]{1,0:T(8,128)(2,1)} %param.5) | copy-start | bytes 12292
Sparse Core Ops, SparseCore 0:
  13.4 480.2 all-reduce.8
where the time goes:
time: 2310 us
  blocking collectives  2270 us (98%)
  between operations  24.6 us (1%)
    psum x2, blocking collectives, on_device(): lax.psum((part_c, own_gram_a, own_gram_b), 'wide')  834 us
    psum x4, blocking collectives, combine_dot(): return lax.psum(wide_part, 'wide') + lax.psum(narrow_part, 'narrow')  706 us
    psum x1, blocking collectives, gram_product(): cross_a, cross_b = lax.psum((local_a, local_b), 'wide')  412 us
    all_gather x1, blocking collectives, on_device(): lax.all_gather(factor_b, 'wide', axis=1, tiled=True)  129 us
    psum x2, blocking collectives, gram_product(): cross_c = lax.psum(local_c, 'narrow')  122 us
    psum x1, blocking collectives, on_device(): mttkrp_a, gram_c = lax.psum((part_a, own_gram_c), 'narrow')  66.7 us
  transfers between devices with their start and end apart: 1, of which 0 were waited for; matrix products, arithmetic and copies ran while one was open for 0% of the time, Pallas kernels for 0%

commit v1 on v0

--- a/solution.py
+++ b/solution.py
@@ -57,7 +57,9 @@
     j_local = factor_b.shape[1]
     flattened = tensor.reshape(k_local * i_local, j_whole)
     contracted = lax.dot_general(
-        lax.all_gather(factor_b, "wide", axis=1, tiled=True),
+        jnp.concatenate(
+            lax.all_to_all(jnp.stack([factor_b] * lax.axis_size("wide")), "wide", 0, 0), axis=1
+        ),
         flattened,
         (((1,), (1,)), ((), ())),
         preferred_element_type=jnp.float32,

time: 2310 us -> 2210 us (0.957)
  blocking collectives: 2270 us -> 2150 us
    all_gather x1 -> x0, blocking collectives: 129 us -> none  [on_device(): lax.all_gather(factor_b, 'wide', axis=1, tiled=True)]
  transfers between devices with their start and end apart: 1 -> 2, of which waited for: 0 -> 0; matrix products, arithmetic and copies ran while one was open for 0% -> 0% of each run, Pallas kernels for 0% -> 0%
where the time goes in v1:
time: 2210 us
  blocking collectives  2150 us (97%)
  between operations  24.7 us (1%)
    psum x2, blocking collectives, on_device(): lax.psum((part_c, own_gram_a, own_gram_b), 'wide')  845 us
    psum x4, blocking collectives, combine_dot(): return lax.psum(wide_part, 'wide') + lax.psum(narrow_part, 'narrow')  706 us
    psum x1, blocking collectives, gram_product(): cross_a, cross_b = lax.psum((local_a, local_b), 'wide')  412 us
    psum x2, blocking collectives, gram_product(): cross_c = lax.psum(local_c, 'narrow')  121 us
    psum x1, blocking collectives, on_device(): mttkrp_a, gram_c = lax.psum((part_a, own_gram_c), 'narrow')  67 us
  transfers between devices with their start and end apart: 2, of which 0 were waited for; matrix products, arithmetic and copies ran while one was open for 0% of the time, Pallas kernels for 0%

profile of v1, /device:TPU:1, one launch (start us, length us, event | category | flops | bytes accessed | tf_op | source)
XLA Modules:
  0.0 2212.4 jit_solution(12543936142673916082)
XLA Ops:
  7.2 1.7 stack.2
  8.9 17.2 all-to-all-start
  26.2 0.7 convert_element_type.12
  26.9 0.7 convert_element_type.11
  27.5 1.6 convolution_bitcast_fusion
  29.5 418.9 %all-reduce.3 = (f32[32,32]{1,0:T(8,128)S(1)}, f32[32,32]{1,0:T(8,128)S(1)}) all-reduce(f32[32,32]{1,0:T(8,128)S(1)} %fusion.48, f32[32,32]{1,0:T(8,128)S(1)} %fusion.51), channel_id=1, replica_groups=mesh['wide'=64,'narrow'=8] {'wide'}, use_global_device_ids=true, to_apply=%region_0.0 | all-reduce | flops 2048 | bytes 16384 | tf_op jit(solution)/shard_map/psum | solution.py:76
  448.8 0.2 reshape.26
  449.0 1.1 fusion.50
  450.1 0.3 fusion.14
  450.4 67.0 %all-reduce.6 = (f32[32,32]{1,0:T(8,128)S(1)}, f32[32,64]{1,0:T(8,128)S(1)}) all-reduce(f32[32,32]{1,0:T(8,128)S(1)} %fusion.49, f32[32,64]{1,0:T(8,128)S(1)} %bitcast.63), channel_id=1, replica_groups=mesh['wide'=64,'narrow'=8] {'narrow'}, use_global_device_ids=true, to_apply=%region_1.0 | all-reduce | flops 3072 | bytes 24576 | tf_op jit(solution)/shard_map/psum | solution.py:75
  517.8 0.8 convolution_subtract_fusion
  519.0 0.3 fusion.12
  519.3 426.1 %all-reduce.2 = (f32[32,2]{0,1:T(2,128)S(1)}, f32[32,32]{1,0:T(8,128)S(1)}, f32[32,32]{1,0:T(8,128)S(1)}) all-reduce(f32[32,2]{0,1:T(2,128)S(1)} %bitcast.64, f32[32,32]{1,0:T(8,128)S(1)} %convolution_bitcast_fusion.6, f32[32,32]{1,0:T(8,128)S(1)} %convolution_bitcast_fusion.4), channel_id=1, replica_groups=mesh['wide'=64,'narrow'=8] {'wide'}, use_global_device_ids=true, to_apply=%region_8.0 | all-reduce | flops 2112 | bytes 16896 | tf_op jit(solution)/shard_map/psum | solution.py:76
  945.8 0.8 multiply_reduce_fusion.7
  946.6 59.8 %all-reduce.5 = (f32[32,32]{1,0:T(8,128)S(1)}, f32[]{:T(128)}, f32[]{:T(128)}) all-reduce(f32[32,32]{1,0:T(8,128)S(1)} %convolution_bitcast_fusion.5, f32[]{:T(128)} %get-tuple-element.8, f32[]{:T(128)} %get-tuple-element.7), channel_id=1, replica_groups=mesh['wide'=64,'narrow'=8] {'narrow'}, use_global_device_ids=true, to_apply=%region_12.0 | all-reduce | flops 1026 | bytes 8208 | tf_op jit(solution)/shard_map/psum | solution.py:38
  1006.4 0.8 multiply_reduce_fusion.3
  1007.3 0.8 multiply_reduce_fusion.2
  1010.6 228.2 %all-reduce.1 = (f32[]{:T(128)}, f32[]{:T(128)}) all-reduce(f32[]{:T(128)S(6)} %add.140, f32[]{:T(128)S(6)} %add.148), channel_id=1, replica_groups=mesh['wide'=64,'narrow'=8] {'wide'}, use_global_device_ids=true, to_apply=%region_7.0 | all-reduce | flops 2 | bytes 16 | tf_op jit(solution)/shard_map/psum | solution.py:20
  1241.4 0.6 multiply_reduce_fusion.1
  1242.0 0.6 multiply_reduce_fusion
  1243.9 0.6 multiply_reduce_fusion.6
  1244.5 210.8 %psum.153 = f32[]{:T(128)} all-reduce(f32[]{:T(128)S(6)} %add.153), channel_id=1, replica_groups=mesh['wide'=64,'narrow'=8] {'wide'}, use_global_device_ids=true, to_apply=%region_21.0 | all-reduce | flops 1 | bytes 8 | tf_op jit(solution)/shard_map/psum | solution.py:20
  1455.4 38.9 %psum.154 = f32[]{:T(128)} all-reduce(f32[]{:T(128)} %multiply_reduce_fusion.6), channel_id=1, replica_groups=mesh['wide'=64,'narrow'=8] {'narrow'}, use_global_device_ids=true, to_apply=%region_23.0 | all-reduce | flops 1 | bytes 8 | tf_op jit(solution)/shard_map/psum | solution.py:20
  1496.5 412.3 %all-reduce = (f32[32,32]{1,0:T(8,128)S(1)}, f32[32,32]{1,0:T(8,128)S(1)}) all-reduce(f32[32,32]{1,0:T(8,128)S(1)} %convolution_bitcast_fusion.3, f32[32,32]{1,0:T(8,128)S(1)} %convolution_bitcast_fusion.1), channel_id=1, replica_groups=mesh['wide'=64,'narrow'=8] {'wide'}, use_global_device_ids=true, to_apply=%region_24.0 | all-reduce | flops 2048 | bytes 16384 | tf_op jit(solution)/shard_map/psum | solution.py:37
  1908.9 0.8 fusion.11
  1909.7 61.5 %all-reduce.4 = (f32[32,32]{1,0:T(8,128)S(1)}, f32[]{:T(128)}) all-reduce(f32[32,32]{1,0:T(8,128)S(1)} %convolution_bitcast_fusion.2, f32[]{:T(128)} %fusion.11), channel_id=1, replica_groups=mesh['wide'=64,'narrow'=8] {'narrow'}, use_global_device_ids=true, to_apply=%region_25.0 | all-reduce | flops 1025 | bytes 8200 | tf_op jit(solution)/shard_map/psum | solution.py:38
  1971.2 0.7 fusion.9
  1972.0 0.7 fusion.10
  1974.0 228.4 %psum.158 = f32[]{:T(128)} all-reduce(f32[]{:T(128)S(6)} %add.164), channel_id=1, replica_groups=mesh['wide'=64,'narrow'=8] {'wide'}, use_global_device_ids=true, to_apply=%region_29.0 | all-reduce | flops 1 | bytes 8 | tf_op jit(solution)/shard_map/psum | solution.py:20
  2203.8 0.6 multiply_add_fusion.1
  2204.4 0.6 multiply_add_fusion
  2205.0 0.6 multiply_add_fusion.4
  (36 shorter events, 3.0 us)
Async XLA Ops:
  7.2 20.4 copy-start
  8.9 439.7 %all-to-all-start = ((bf16[64,32,128]{2,1,0:T(8,128)(2,1)}), bf16[64,32,128]{2,1,0:T(8,128)(2,1)S(1)}, u32[]{:S(2)}, u32[]{:S(2)}) async-start(bf16[64,32,128]{2,1,0:T(8,128)(2,1)} %stack.2), calls=%async_computation | async-start | bytes 1048576 | tf_op jit(solution)/shard_map/all_to_all | solution.py:61
  26.1 491.7 %all-reduce.9.cloned.1.call-start = ((), (), s32[]{:S(2)}) async-start(), calls=%async_computation.1 | async-start | bytes 2097152 | tf_op jit(solution)/shard_map/psum | solution.py:83
  27.5 1.6 copy-start.3
  27.5 1.7 copy-start.1
  27.5 1.8 copy-start.2
Sparse Core Ops, SparseCore 0:
  32.4 473.5 all-reduce.8
